TPU v7x, 256 devices: a whole 4x4x8 slice. The times are simulated.
256 devices in a mesh: seq: 32 (over y, x, core), tp: 8 (over z).
Axes of the slice: x: 4, y: 4, z: 8, core: 2. Of those that a mesh axis runs over, the one named last changes fastest.
Arguments:
- queries: bfloat16 [32, 64, 4096], P('seq', None, 'tp'), may hold values from -8 to 8
- draft_kv: bfloat16 [32, 64, 8, 128], P('seq', None, 'tp'), may hold values from -12.5 to 12.5
- cache_kv: bfloat16 [8, 16384, 8, 128], P(None, 'seq', 'tp'), may hold values from -10 to 10
- cache_len: int32 [8], replicated, may hold values from 4096 to 16384
- group_of: int32 [32], replicated, may hold values from 0 to 7, as said below
- parents: int32 [32, 64], P('seq'), may hold values from 0 to 62, as said below
- sink_logit: float32 [64], P('tp'), may hold values from 4 to 20
- w_out: bfloat16 [4096, 2880], P('tp'), may hold values from -0.09375 to 0.09375
- hidden_in: bfloat16 [2048, 2880], P('seq', 'tp'), may hold values from -3 to 3
- norm_gain: float32 [2880], replicated, may hold values from 0.5 to 1.5
- routes: int32 [2048, 4], P('seq'), may hold values from 0 to 31, all different within a row; in each aligned block of 64 rows (0 to 63, 64 to 127, ...) at most 16 rows name the same one
- route_weight: float32 [2048, 4], P('seq'), may hold values from 0.1 to 1
- w_gate_up: bfloat16 [32, 2, 2880, 2880], P('seq', None, None, 'tp'), may hold values from -0.109375 to 0.109375
- w_down: bfloat16 [32, 2880, 2880], P('seq', 'tp'), may hold values from -0.109375 to 0.109375
- accepted_idx: int32 [32, 16], P('seq'), may hold values from 0 to 45, as said below
- accepted_len: int32 [32], P('seq'), may hold values from 1 to 16, as said below
- tail_slot: int32 [32], replicated, may hold values from 0 to 31, each once
Outputs:
- out_hidden: bfloat16 [2048, 2880], P('seq', 'tp')
- new_tail: bfloat16 [32, 16, 8, 128], P('seq', None, 'tp')
Inputs may be any that keep to these rules, and one draw needn't show every extreme that they name: `parents`: node 0 of every tree is its root and its own parent; every other node's parent is one of the three nodes before it. `accepted_idx`: row r lists the first 16 nodes of a path from the root of request r's tree down to one of its last four nodes, root first. `accepted_len`: each request accepts one or more nodes. `group_of`: every prompt group has exactly 4 requests. `routes`: the 4 experts of a token differ; at most 16 of one device's rows (one aligned block of 64 tokens) name one expert.
All inputs are finite; a program needn't handle non-finite values.
Results may differ from a plain program's by a relative error of at most 0.025.
Values may be sent and summed in bfloat16 or wider, within the bound.
A program may use at most 128 MiB of HBM per device.

v0:
```python
import jax
import jax.numpy as jnp
from jax import lax
from jax.sharding import PartitionSpec as P

HQ = 64
KVH = 8
HD = 64


def ancestry(parents):
    tree_len = parents.shape[1]
    node_ids = jnp.arange(tree_len, dtype=jnp.int32)
    linked = (parents[:, :, None] == node_ids[None, None, :]) | (
        node_ids[:, None] == node_ids[None, :]
    )[None]
    reachable = linked.astype(jnp.float32)
    for repeat in range((tree_len - 1).bit_length()):
        reachable = jnp.minimum(
            jnp.einsum("rij,rjk->rik", reachable, reachable, precision=lax.Precision.HIGHEST), 1.0
        )
    return reachable


def cache_block(block_queries, block_groups, cache_kv, cache_len, positions):
    block_rows, tree_len, head_cols = block_queries.shape
    kv_dev = cache_kv.shape[2]
    grouped = block_queries.reshape(block_rows, tree_len, kv_dev, HQ // KVH, HD)
    picked = jnp.take(cache_kv, block_groups, axis=0)
    cache_keys = picked[..., :HD]
    cache_values = picked[..., HD:]
    scores = (
        jnp.einsum("rtkqd,rckd->rkqtc", grouped, cache_keys, preferred_element_type=jnp.float32)
        * 0.125
    )
    lengths = jnp.take(cache_len, block_groups)
    usable = (positions[None, :] < lengths[:, None])[:, None, None, None, :]
    masked = jnp.where(usable, scores, -1e30)
    shard_max = jnp.max(masked, axis=-1)
    weights = jnp.where(usable, jnp.exp(masked - shard_max[..., None]), 0.0)
    shard_sum = jnp.sum(weights, axis=-1)
    shard_out = jnp.einsum(
        "rkqtc,rckd->rkqtd",
        weights.astype(jnp.bfloat16),
        cache_values,
        preferred_element_type=jnp.float32,
    )
    shard_out = (shard_out / jnp.maximum(shard_sum, 1.0)[..., None]).astype(jnp.bfloat16)
    out_rows = shard_out.transpose(0, 3, 1, 2, 4).reshape(block_rows, tree_len, head_cols)
    max_rows = shard_max.transpose(0, 3, 1, 2).reshape(block_rows, tree_len, -1)
    sum_rows = shard_sum.transpose(0, 3, 1, 2).reshape(block_rows, tree_len, -1)
    return (out_rows, max_rows, sum_rows)


def expert_rows(arrived, w_gate_up, w_down):
    exp_dev = w_gate_up.shape[0]
    sources = arrived.shape[0] // exp_dev
    grouped = arrived.reshape(sources, exp_dev, arrived.shape[1], arrived.shape[2])
    gate_proj = jnp.einsum(
        "sexd,edf->sexf", grouped, w_gate_up[:, 0], preferred_element_type=jnp.float32
    )
    upward = jnp.einsum(
        "sexd,edf->sexf", grouped, w_gate_up[:, 1], preferred_element_type=jnp.float32
    )
    active = (gate_proj * jax.nn.sigmoid(1.702 * gate_proj) * (upward + 1.0)).astype(jnp.bfloat16)
    down_part = jnp.einsum("sexf,efd->sexd", active, w_down, preferred_element_type=jnp.float32)
    return down_part.reshape(arrived.shape[0], arrived.shape[1], -1)


def shards(
    queries,
    draft_kv,
    cache_kv,
    cache_len,
    group_of,
    parents,
    sink_logit,
    w_out,
    hidden_in,
    norm_gain,
    routes,
    route_weight,
    w_gate_up,
    w_down,
    accepted_idx,
    accepted_len,
    tail_slot,
):
    seq_count = lax.axis_size("seq")
    req_dev, tree_len, head_cols = queries.shape
    kv_dev = cache_kv.shape[2]
    per_kv = HQ // KVH
    heads_dev = kv_dev * per_kv
    shard_len = cache_kv.shape[1]
    positions = lax.axis_index("seq") * shard_len + jnp.arange(shard_len, dtype=jnp.int32)
    every_query = lax.all_gather(queries, "seq", axis=0, tiled=True)
    requests_all = every_query.shape[0]
    block_count = requests_all // 8
    stacked = (
        every_query.reshape(block_count, 8, tree_len, head_cols),
        group_of.reshape(block_count, 8),
    )
    shard_out, shard_max, shard_sum = lax.map(
        lambda blocks: cache_block(blocks[0], blocks[1], cache_kv, cache_len, positions), stacked
    )
    shard_out = shard_out.reshape(seq_count, req_dev, tree_len, head_cols)
    shard_max = shard_max.reshape(seq_count, req_dev, tree_len, heads_dev)
    shard_sum = shard_sum.reshape(seq_count, req_dev, tree_len, heads_dev)
    came_out = lax.all_to_all(shard_out, "seq", split_axis=0, concat_axis=0, tiled=True)
    came_max, came_sum = (
        lax.all_to_all(shard_max, "seq", split_axis=0, concat_axis=0, tiled=True),
        lax.all_to_all(shard_sum, "seq", split_axis=0, concat_axis=0, tiled=True),
    )
    reachable = ancestry(parents)
    own_heads = queries.reshape(req_dev, tree_len, kv_dev, per_kv, HD)
    draft_keys = draft_kv[..., :HD]
    draft_values = draft_kv[..., HD:]
    tree_scores = (
        jnp.einsum("rtkqd,rukd->rkqtu", own_heads, draft_keys, preferred_element_type=jnp.float32)
        * 0.125
    )
    allowed = (reachable > 0.5)[:, None, None, :, :]
    tree_masked = jnp.where(allowed, tree_scores, -1e30)
    tree_max = jnp.max(tree_masked, axis=-1)
    tree_weight = jnp.where(allowed, jnp.exp(tree_masked - tree_max[..., None]), 0.0)
    tree_sum = jnp.sum(tree_weight, axis=-1)
    tree_num = jnp.einsum(
        "rkqtu,rukd->rkqtd",
        tree_weight.astype(jnp.bfloat16),
        draft_values,
        preferred_element_type=jnp.float32,
    )
    tree_max = tree_max.transpose(0, 3, 1, 2).reshape(req_dev, tree_len, heads_dev)
    tree_sum = tree_sum.transpose(0, 3, 1, 2).reshape(req_dev, tree_len, heads_dev)
    tree_num = tree_num.transpose(0, 3, 1, 2, 4).reshape(req_dev, tree_len, heads_dev, HD)
    sink_rows = sink_logit[None, None, :]
    ceiling = jnp.maximum(jnp.maximum(jnp.max(came_max, axis=0), tree_max), sink_rows)
    shard_scale = came_sum * jnp.exp(came_max - ceiling[None])
    tree_scale = jnp.exp(tree_max - ceiling)
    denominator = (
        jnp.sum(shard_scale, axis=0) + tree_scale * tree_sum + jnp.exp(sink_rows - ceiling)
    )
    weighted = jnp.sum(
        shard_scale[..., None]
        * came_out.reshape(seq_count, req_dev, tree_len, heads_dev, HD).astype(jnp.float32),
        axis=0,
    )
    numerator = weighted + tree_scale[..., None] * tree_num
    attention = (
        (numerator / denominator[..., None])
        .reshape(req_dev * tree_len, heads_dev * HD)
        .astype(jnp.bfloat16)
    )
    projected = jnp.dot(attention, w_out, preferred_element_type=jnp.float32)
    width_dev = hidden_in.shape[1]
    tp_index = lax.axis_index("tp")
    summed = lax.psum(projected, "tp")
    resid_full = lax.all_gather(hidden_in, "tp", axis=1, tiled=True)
    stream = (resid_full.astype(jnp.float32) + summed).astype(jnp.bfloat16)
    stream_f = stream.astype(jnp.float32)
    inv_scale = lax.rsqrt(jnp.mean(stream_f * stream_f, axis=-1, keepdims=True) + 1e-05)
    normed_full = (stream_f * inv_scale * norm_gain[None, :]).astype(jnp.bfloat16)
    stream_cols = lax.dynamic_slice_in_dim(stream, tp_index * width_dev, width_dev, 1)
    tok_dev = routes.shape[0]
    top_count = routes.shape[1]
    exp_dev = w_gate_up.shape[0]
    experts_all = seq_count * exp_dev
    capacity = 2 * tok_dev * top_count // experts_all
    flat_routes = routes.reshape(-1)
    onehot = (flat_routes[:, None] == jnp.arange(experts_all, dtype=jnp.int32)[None, :]).astype(
        jnp.int32
    )
    position = jnp.sum((jnp.cumsum(onehot, axis=0) - onehot) * onehot, axis=1)
    slot_ids = flat_routes * capacity + position
    buckets = jnp.arange(experts_all * capacity, dtype=jnp.int32)
    placing = jnp.sum(
        (slot_ids.reshape(tok_dev, top_count)[None, :, :] == buckets[:, None, None]).astype(
            jnp.int32
        ),
        axis=2,
    ).astype(jnp.bfloat16)
    dispatched = (
        jnp.dot(placing, normed_full, preferred_element_type=jnp.float32)
        .astype(jnp.bfloat16)
        .reshape(experts_all, capacity, -1)
    )
    down_part = expert_rows(
        lax.all_to_all(dispatched, "seq", split_axis=0, concat_axis=0, tiled=True),
        w_gate_up,
        w_down,
    )
    expert_out = lax.psum_scatter(
        down_part.astype(jnp.bfloat16), "tp", scatter_dimension=2, tiled=True
    )
    returned = lax.all_to_all(expert_out, "seq", split_axis=0, concat_axis=0, tiled=True)
    gathered_rows = jnp.take(
        returned.reshape(experts_all * capacity, -1), slot_ids, axis=0
    ).reshape(tok_dev, top_count, -1)
    mixture = jnp.sum(route_weight[:, :, None] * gathered_rows.astype(jnp.float32), axis=1)
    out_hidden = (stream_cols.astype(jnp.float32) + mixture).astype(jnp.bfloat16)
    blk_len = accepted_idx.shape[1]
    chosen = draft_kv[jnp.arange(req_dev, dtype=jnp.int32)[:, None], accepted_idx]
    kept_rows = jnp.arange(blk_len, dtype=jnp.int32)[None, :] < accepted_len[:, None]
    picked_rows = jnp.where(kept_rows[:, :, None, None], chosen, jnp.zeros_like(chosen))
    everyone = lax.all_gather(picked_rows, "seq", axis=0, tiled=True)
    my_slots = lax.axis_index("seq") * req_dev + jnp.arange(req_dev, dtype=jnp.int32)
    selector = (tail_slot[None, :] == my_slots[:, None]).astype(jnp.bfloat16)
    new_tail = jnp.dot(
        selector, everyone.reshape(everyone.shape[0], -1), preferred_element_type=jnp.float32
    ).astype(jnp.bfloat16)
    new_tail = new_tail.reshape(req_dev, blk_len, kv_dev, -1)
    return (out_hidden, new_tail)


def solution(mesh):
    in_specs = (
        P("seq", None, "tp"),
        P("seq", None, "tp", None),
        P(None, "seq", "tp", None),
        P(),
        P(),
        P("seq", None),
        P("tp"),
        P("tp", None),
        P("seq", "tp"),
        P(),
        P("seq", None),
        P("seq", None),
        P("seq", None, None, "tp"),
        P("seq", "tp", None),
        P("seq", None),
        P("seq"),
        P(),
    )
    out_specs = (P("seq", "tp"), P("seq", None, "tp", None))
    return jax.shard_map(shards, mesh=mesh, in_specs=in_specs, out_specs=out_specs, check_vma=False)
```

profile of v0, /device:TPU:1, one launch (start us, length us, event | category | flops | bytes accessed | tf_op | source)
XLA Modules:
  0.0 533.3 jit_solution(3878875501359007208)
XLA Ops:
  10.3 53.3 %all-gather.3.cloned.1.call-done = bf16[32,64,512]{2,1,0:T(8,128)(2,1)} async-done(((bf16[1,64,512]{2,1,0:T(8,128)(2,1)}), bf16[32,64,512]{2,1,0:T(8,128)(2,1)}) %all-gather.3.cloned.1.call-update) | async-done | bytes 2097168 | tf_op jit(solution)/shard_map/all_gather | solution.py:96
  63.7 97.3 %while.15 = (s32[]{:T(128)}, bf16[4,8,64,512]{3,2,1,0:T(8,128)(2,1)}, f32[4,8,64,8]{2,3,1,0:T(8,128)}, f32[4,8,64,8]{2,3,1,0:T(8,128)}, s32[4,8]{1,0:T(4,128)S(1...) while((s32[]{:T(128)}, ...), condition=%wide.region_3.4_spmd.clone, body=%wide.region_0.3_spmd.clone.sunk | while | flops 565184128 | bytes 43791872 | solution.py:103
  65.0 2.9 gather_fusion.1
  67.9 2.3 copy.129
  70.2 2.4 bitcast_select_fusion.4
  75.3 2.7 bitcast_reduce_fusion.3
  78.0 2.3 fusion.128
  80.9 2.6 fusion.129
  89.4 2.9 gather_fusion.1
  92.3 2.3 copy.129
  94.5 2.4 bitcast_select_fusion.4
  99.6 2.7 bitcast_reduce_fusion.3
  102.3 2.3 fusion.128
  105.3 2.6 fusion.129
  113.7 2.9 gather_fusion.1
  116.6 2.3 copy.129
  118.9 2.4 bitcast_select_fusion.4
  124.0 2.7 bitcast_reduce_fusion.3
  126.7 2.3 fusion.128
  129.6 2.6 fusion.129
  138.0 2.9 gather_fusion.1
  143.2 2.4 bitcast_select_fusion.4
  148.3 2.7 bitcast_reduce_fusion.3
  151.0 2.3 fusion.128
  153.9 2.6 fusion.129
  162.7 5.1 all-to-all-start.1
  170.4 4.7 all-to-all-done.1
  175.1 3.9 all-to-all-start
  180.8 5.6 %all-to-all-done = f32[32,1,512]{2,1,0:T(1,128)S(1)} async-done(((f32[32,1,512]{2,1,0:T(1,128)}), f32[32,1,512]{2,1,0:T(1,128)S(1)}, u32[]{:S(2)}, u32[]{:S(2)}) %all-to-all-start) | async-done | bytes 65568 | tf_op jit(solution)/shard_map/all_to_all | solution.py:112
  186.4 4.7 all-to-all-start.2
  193.3 23.3 %all-gather = bf16[8,360,64]{1,2,0:T(8,128)(2,1)S(1)} all-gather(bf16[1,360,64]{1,2,0:T(8,128)(2,1)} %bitcast.318), channel_id=1, replica_groups=mesh['seq'=32,'tp'=8] {'tp'}, dimensions={0}, use_global_device_ids=true | all-gather | bytes 414720 | tf_op jit(solution)/shard_map/all_gather | solution.py:158
  227.4 5.9 %mul.135 = f32[32,64,8,64]{3,2,1,0:T(8,128)} broadcast(f32[32,64,8]{2,1,0:T(8,128)} %copy.92), dimensions={0,1,2} | broadcast | bytes 4259840 | tf_op jit(solution)/shard_map/mul | solution.py:144
  233.4 7.5 %mul.136 = f32[32,1,64,512]{3,2,1,0:T(8,128)} reshape(f32[32,64,8,64]{3,2,1,0:T(8,128)} %mul.135) | data formatting | bytes 8388608 | tf_op jit(solution)/shard_map/mul | solution.py:144
  240.9 3.6 multiply_reduce_fusion
  247.8 72.6 %all-reduce.3.cloned.1.call-done = f32[64,2880]{1,0:T(8,128)} async-done(((f32[64,2880]{1,0:T(8,128)}), f32[64,2880]{1,0:T(8,128)}) %all-reduce.3.cloned.1.call-update) | async-done | bytes 737296 | tf_op jit(solution)/shard_map/psum | solution.py:157
  322.7 2.7 convolution_convert_fusion.1
  325.4 4.6 copy.103
  329.9 50.3 %all_to_all.25 = bf16[32,16,2880]{2,1,0:T(8,128)(2,1)S(1)} all-to-all(bf16[32,16,2880]{2,1,0:T(8,128)(2,1)} %bitcast.309), channel_id=1, replica_groups=mesh['seq'=32,'tp'=8] {'seq'}, dimensions={0} | all-to-all | bytes 5898240 | tf_op jit(solution)/shard_map/all_to_all | solution.py:188
  381.9 4.2 fusion.27
  386.1 8.5 %convolution_convert_fusion = bf16[32,16,2880]{2,1,0:T(8,128)(2,1)} fusion(bf16[1,360,2880]{2,1,0:T(8,128)(2,1)} %param.32, bf16[32,16,2880]{2,1,0:T(8,128)(2,1)} %copy-done.2, bf16[1,2,2880,360]{2,3,1,0:T(8,128)(2,1)} %param.31, f32[32,1,16,360]{3,2,0,1:T(8,128)} %fusion.27), kind=kOutput, calls=%fused_computation.40 | convolution fusion | flops 2126315520 | bytes 10989568 | tf_op jit(solution)/shard_map/sexf,efd->sexd/dot_general | solution.py:66
  394.6 21.4 %copy.108 = bf16[32,16,2880]{1,0,2:T(8,128)(2,1)} copy(bf16[32,16,2880]{2,1,0:T(8,128)(2,1)} %convolution_convert_fusion) | data formatting | bytes 5898240
  416.0 39.5 %reshape.749 = bf16[2880,512]{1,0:T(8,128)(2,1)} reshape(bf16[2880,32,16]{2,1,0:T(8,128)(2,1)} %bitcast.306) | data formatting | bytes 5898240
  457.1 22.6 %all_gather.11 = bf16[32,16,1,128]{3,1,2,0:T(8,128)(2,1)S(1)} all-gather(bf16[1,16,1,128]{3,1,2,0:T(8,128)(2,1)S(1)} %bitcast_select_fusion.2), channel_id=1, replica_groups=mesh['seq'=32,'tp'=8] {'seq'}, dimensions={0}, use_global_device_ids=true | all-gather | bytes 135168 | tf_op jit(solution)/shard_map/all_gather | solution.py:205
  479.9 12.3 %reduce-scatter.4.cloned.1.call-done = bf16[360,512]{1,0:T(8,128)(2,1)} async-done(((bf16[2880,512]{1,0:T(8,128)(2,1)}), bf16[360,512]{1,0:T(8,128)(2,1)}) %reduce-scatter.4.cloned.1.call-update) | async-done | bytes 368656
  492.2 4.4 reshape.750
  496.5 5.0 copy.109
  501.6 11.1 %all-to-all-start.4 = ((bf16[32,16,360]{2,1,0:T(8,128)(2,1)}), bf16[32,16,360]{2,1,0:T(8,128)(2,1)S(1)}, u32[]{:S(2)}, u32[]{:S(2)}) async-start(bf16[32,16,360]{2,1,0:T(8,128)(2,1)} %copy.109), calls=%async_computation.4 | async-start | bytes 786432 | tf_op jit(solution)/shard_map/all_to_all | solution.py:195
  514.1 8.7 %all-to-all-done.4 = bf16[32,16,360]{2,1,0:T(8,128)(2,1)S(1)} async-done(((bf16[32,16,360]{2,1,0:T(8,128)(2,1)}), bf16[32,16,360]{2,1,0:T(8,128)(2,1)S(1)}, u32[]{:S(2)}, u32[]{:S(2)}) %all-to-all-start.4) | async-done | bytes 368672 | tf_op jit(solution)/shard_map/all_to_all | solution.py:195
  (178 shorter events, 74.3 us)
Async XLA Ops:
  7.2 237.3 %copy-start = (bf16[512,2880]{0,1:T(8,128)(2,1)S(1)}, bf16[512,2880]{0,1:T(8,128)(2,1)}, u32[]{:S(2)}) copy-start(bf16[512,2880]{0,1:T(8,128)(2,1)} %param.26) | copy-start | bytes 8847364
  7.2 56.5 %all-gather.3.cloned.1.call-start = ((), (), s32[]{:S(2)}) async-start(), calls=%async_computation.6 | async-start | bytes 2162688 | tf_op jit(solution)/shard_map/all_gather | solution.py:96
  63.7 115.5 %copy-start.6 = (bf16[1,64,512]{2,1,0:T(8,128)(2,1)S(1)}, bf16[1,64,512]{2,1,0:T(8,128)(2,1)}, u32[]{:S(2)}) copy-start(bf16[1,64,512]{2,1,0:T(8,128)(2,1)} %param.19) | copy-start | bytes 196612
  63.7 115.6 %copy-start.13 = (s32[64,4]{0,1:T(4,128)S(1)}, s32[64,4]{0,1:T(4,128)}, u32[]{:S(2)}) copy-start(s32[64,4]{0,1:T(4,128)} %param.29) | copy-start | bytes 3076
  78.0 3.0 copy-start.1
  102.3 3.0 copy-start.1
  126.6 3.0 copy-start.1
  150.9 3.0 copy-start.1
  161.0 30.9 %copy-start.7 = (bf16[1,64,1,128]{3,1,2,0:T(8,128)(2,1)S(1)}, bf16[1,64,1,128]{3,1,2,0:T(8,128)(2,1)}, u32[]{:S(2)}) copy-start(bf16[1,64,1,128]{3,1,2,0:T(8,128)(2,1)} %param.20) | copy-start | bytes 49156
  162.7 12.4 %all-to-all-start.1 = ((f32[32,1,512]{2,1,0:T(1,128)}), f32[32,1,512]{2,1,0:T(1,128)S(1)}, u32[]{:S(2)}, u32[]{:S(2)}) async-start(f32[32,1,512]{2,1,0:T(1,128)} %reshape.754), calls=%async_computation.1 | async-start | bytes 131072 | tf_op jit(solution)/shard_map/all_to_all | solution.py:111
  175.1 17.0 %copy-start.9 = (f32[32,1,512]{2,1,0:T(1,128)}, f32[32,1,512]{2,1,0:T(1,128)S(1)}, u32[]{:S(2)}) copy-start(f32[32,1,512]{2,1,0:T(1,128)S(1)} %all-to-all-done.1) | copy-start | bytes 196612
  175.1 11.3 %all-to-all-start = ((f32[32,1,512]{2,1,0:T(1,128)}), f32[32,1,512]{2,1,0:T(1,128)S(1)}, u32[]{:S(2)}, u32[]{:S(2)}) async-start(f32[32,1,512]{2,1,0:T(1,128)} %reshape.752), calls=%async_computation | async-start | bytes 131072 | tf_op jit(solution)/shard_map/all_to_all | solution.py:112
  186.4 4.8 copy-start.11
  186.4 54.4 %all-to-all-start.2 = ((bf16[32,1,64,512]{3,2,1,0:T(8,128)(2,1)}), bf16[32,1,64,512]{3,2,1,0:T(8,128)(2,1)}, u32[]{:S(2)}, u32[]{:S(2)}) async-start(bf16[32,1,64,512]{3,2,1,0:T(8,128)(2,1)} %bitcast.313), calls=%async_computation.2 | async-start | bytes 4194304 | tf_op jit(solution)/shard_map/all_to_all | solution.py:109
  191.2 129.2 %all-reduce.3.cloned.1.call-start = ((), (), s32[]{:S(2)}) async-start(), calls=%async_computation.7 | async-start | bytes 1507328 | tf_op jit(solution)/shard_map/psum | solution.py:157
  192.4 28.8 %copy-start.10 = (f32[32,1,512]{2,1,0:T(1,128)S(1)}, f32[32,1,512]{2,1,0:T(1,128)}, u32[]{:S(2)}) copy-start(f32[32,1,512]{2,1,0:T(1,128)} %copy-done.9) | copy-start | bytes 196612
  193.3 28.8 %copy-start.12 = (f32[32,1,512]{2,1,0:T(1,128)S(1)}, f32[32,1,512]{2,1,0:T(1,128)}, u32[]{:S(2)}) copy-start(f32[32,1,512]{2,1,0:T(1,128)} %copy-done.11) | copy-start | bytes 196612
  240.9 3.6 copy-start.4
  240.9 3.6 copy-start.5
  244.5 2.0 copy-start.16
  244.5 2.8 copy-start.15
  244.5 78.2 %copy-start.14 = (f32[2880]{0:T(1024)S(1)}, f32[2880]{0:T(1024)}, u32[]{:S(2)}) copy-start(f32[2880]{0:T(1024)} %param.28) | copy-start | bytes 34564
  246.4 245.7 %reduce-scatter.4.cloned.1.call-start = ((), (), s32[]{:S(2)}) async-start(), calls=%async_computation.8 | async-start | bytes 3317760
  321.9 0.8 copy-start.3
  380.2 1.6 copy-start.2
  455.4 0.9 copy-start.19
  455.4 1.0 copy-start.8
  455.4 24.3 %copy-start.18 = (s32[32]{0:T(128)S(1)}, s32[32]{0:T(128)}, u32[]{:S(2)}) copy-start(s32[32]{0:T(128)} %param.35) | copy-start | bytes 388
  479.8 33.0 %copy-start.17 = (f32[64,4]{0,1:T(4,128)S(1)}, f32[64,4]{0,1:T(4,128)}, u32[]{:S(2)}) copy-start(f32[64,4]{0,1:T(4,128)} %param.30) | copy-start | bytes 3076
  501.6 21.3 %all-to-all-start.4 = ((bf16[32,16,360]{2,1,0:T(8,128)(2,1)}), bf16[32,16,360]{2,1,0:T(8,128)(2,1)S(1)}, u32[]{:S(2)}, u32[]{:S(2)}) async-start(bf16[32,16,360]{2,1,0:T(8,128)(2,1)} %copy.109), calls=%async_computation.4 | async-start | bytes 786432 | tf_op jit(solution)/shard_map/all_to_all | solution.py:195
Sparse Core Ops, SparseCore 0:
  10.6 53.0 all-gather.2
  246.5 73.8 all-reduce.2
  455.6 36.5 reduce-scatter.3
where the time goes:
time: 536 us; the launch traced here: 533 us
  local copies, waits for them, and re-layouts  164 us (31%)
  waiting for transfers between devices  158 us (29%)
  blocking collectives  96.2 us (18%)
  matrix products  42.4 us (8%)
  other arithmetic  32.4 us (6%)
  starting transfers between devices  25 us (5%)
  between operations  14.9 us (3%)
    unnamed x48, local copies, waits for them, and re-layouts  77 us
    psum x1, waiting for transfers between devices, shards(): summed = lax.psum(projected, 'tp')  72.6 us
    all_gather x1, waiting for transfers between devices, shards(): every_query = lax.all_gather(queries, 'seq', axis=0, tiled=True)  53.3 us
    all_to_all x1, blocking collectives, shards(): lax.all_to_all(dispatched, 'seq', split_axis=0, concat_axis=0, tiled=True)  50.3 us
    all_gather x1, blocking collectives, shards(): resid_full = lax.all_gather(hidden_in, 'tp', axis=1, tiled=True)  23.3 us
    all_gather x1, blocking collectives, shards(): everyone = lax.all_gather(picked_rows, 'seq', axis=0, tiled=True)  22.6 us
    gather x8, local copies, waits for them, and re-layouts, cache_block(): picked = jnp.take(cache_kv, block_groups, axis=0)  20.7 us
    mul x3, local copies, waits for them, and re-layouts, shards(): shard_scale[..., None]  14.9 us
  transfers between devices with their start and end apart: 7, of which 6 were waited for; matrix products, arithmetic and copies ran while one was open for 7% of the time, Pallas kernels for 0%

commit v1 on v0

--- a/solution.py
+++ b/solution.py
@@ -6,6 +6,28 @@
 HQ = 64
 KVH = 8
 HD = 64
+
+
+def in_order(blocks, dim):
+    shape = list(blocks.shape[1:])
+    shape[dim] *= blocks.shape[0]
+    return jnp.moveaxis(blocks, 0, dim).reshape(shape)
+
+
+def gather_around(value, axis, dim):
+    size = lax.axis_size(axis)
+    pairs = [(i, (i + 1) % size) for i in range(size)]
+    back = [(b, a) for a, b in pairs]
+    lower, upper = ([], [])
+    for step in range(size - 1):
+        if step % 2 == 0:
+            lower.append(lax.ppermute(lower[-1] if lower else value, axis, pairs))
+        else:
+            upper.append(lax.ppermute(upper[-1] if upper else value, axis, back))
+    blocks = jnp.stack([*lower[::-1], value, *upper])
+    shift = lax.axis_index(axis) - len(lower)
+    blocks = blocks[(jnp.arange(size) - shift) % size]
+    return in_order(blocks, dim)
 
 
 def ancestry(parents):
@@ -155,7 +177,7 @@
     width_dev = hidden_in.shape[1]
     tp_index = lax.axis_index("tp")
     summed = lax.psum(projected, "tp")
-    resid_full = lax.all_gather(hidden_in, "tp", axis=1, tiled=True)
+    resid_full = gather_around(hidden_in, "tp", 1)
     stream = (resid_full.astype(jnp.float32) + summed).astype(jnp.bfloat16)
     stream_f = stream.astype(jnp.float32)
     inv_scale = lax.rsqrt(jnp.mean(stream_f * stream_f, axis=-1, keepdims=True) + 1e-05)

time: 536 us -> 515 us (0.961)
  waiting for transfers between devices: 158 us -> 130 us
  blocking collectives: 96.2 us -> 72.9 us
  starting transfers between devices: 25 us -> 39.2 us
  local copies, waits for them, and re-layouts: 164 us -> 178 us
    all_gather x1 -> x0, blocking collectives: 23.3 us -> none  [shards(): resid_full = lax.all_gather(hidden_in, 'tp', axis=1, tiled=True)]
    ppermute x0 -> x7, starting transfers between devices: none -> 14 us  [the longest x3 10.2 us: gather_around(): upper.append(lax.ppermute(upper[-1] if upper else value, axis, back))]
    all_gather x1, waiting for transfers between devices: 53.3 us -> 39.4 us  [shards(): every_query = lax.all_gather(queries, 'seq', axis=0, tiled=True)]
    psum x1, waiting for transfers between devices: 72.6 us -> 60.7 us  [shards(): summed = lax.psum(projected, 'tp')]
    unnamed x48 -> x47, local copies, waits for them, and re-layouts: 77 us -> 87.6 us
  transfers between devices with their start and end apart: 7 -> 14, of which waited for: 6 -> 6; matrix products, arithmetic and copies ran while one was open for 7% -> 31% of each run, Pallas kernels for 0% -> 0%
where the time goes in v1:
time: 515 us; the launch traced here: 512 us
  local copies, waits for them, and re-layouts  178 us (35%)
  waiting for transfers between devices  130 us (25%)
  blocking collectives  72.9 us (14%)
  matrix products  43.1 us (8%)
  starting transfers between devices  39.2 us (8%)
  other arithmetic  34.5 us (7%)
  between operations  14.9 us (3%)
    unnamed x47, local copies, waits for them, and re-layouts  87.6 us
    psum x1, waiting for transfers between devices, shards(): summed = lax.psum(projected, 'tp')  60.7 us
    all_to_all x1, blocking collectives, shards(): lax.all_to_all(dispatched, 'seq', split_axis=0, concat_axis=0, tiled=True)  50.3 us
    all_gather x1, waiting for transfers between devices, shards(): every_query = lax.all_gather(queries, 'seq', axis=0, tiled=True)  39.4 us
    all_gather x1, blocking collectives, shards(): everyone = lax.all_gather(picked_rows, 'seq', axis=0, tiled=True)  22.6 us
    gather x8, local copies, waits for them, and re-layouts, cache_block(): picked = jnp.take(cache_kv, block_groups, axis=0)  20.7 us
    mul x3, local copies, waits for them, and re-layouts, shards(): shard_scale[..., None]  14.9 us
    unnamed x4, waiting for transfers between devices  13 us
  transfers between devices with their start and end apart: 14, of which 6 were waited for; matrix products, arithmetic and copies ran while one was open for 31% of the time, Pallas kernels for 0%

profile of v1, /device:TPU:1, one launch (start us, length us, event | category | flops | bytes accessed | tf_op | source)
XLA Modules:
  0.0 512.0 jit_solution(12104373467268347964)
XLA Ops:
  7.9 2.5 collective-permute-start
  10.5 4.0 collective-permute-start.4
  24.3 39.4 %all-gather.2.cloned.1.call-done = bf16[32,64,512]{2,1,0:T(8,128)(2,1)} async-done(((bf16[1,64,512]{2,1,0:T(8,128)(2,1)}), bf16[32,64,512]{2,1,0:T(8,128)(2,1)}) %all-gather.2.cloned.1.call-update) | async-done | bytes 2097168 | tf_op jit(solution)/shard_map/all_gather | solution.py:118
  63.7 97.2 %while.15 = (s32[]{:T(128)}, bf16[4,8,64,512]{3,2,1,0:T(8,128)(2,1)}, f32[4,8,64,8]{2,3,1,0:T(8,128)}, f32[4,8,64,8]{2,3,1,0:T(8,128)}, s32[4,8]{1,0:T(4,128)S(1...) while((s32[]{:T(128)}, ...), condition=%wide.region_3.4_spmd.clone, body=%wide.region_0.3_spmd.clone.sunk | while | flops 565184128 | bytes 43791872 | solution.py:125
  65.0 2.9 gather_fusion.1
  70.2 2.4 bitcast_select_fusion.4
  75.3 2.7 bitcast_reduce_fusion.3
  78.0 2.3 fusion.128
  80.9 2.6 fusion.129
  89.3 2.9 gather_fusion.1
  94.5 2.4 bitcast_select_fusion.4
  99.6 2.7 bitcast_reduce_fusion.3
  102.3 2.3 fusion.128
  105.2 2.6 fusion.129
  113.7 2.9 gather_fusion.1
  118.8 2.4 bitcast_select_fusion.4
  123.9 2.7 bitcast_reduce_fusion.3
  126.6 2.3 fusion.128
  129.5 2.6 fusion.129
  137.9 2.9 gather_fusion.1
  143.1 2.4 bitcast_select_fusion.4
  148.2 2.7 bitcast_reduce_fusion.3
  150.9 2.3 fusion.128
  153.8 2.6 fusion.129
  162.6 5.1 all-to-all-start.1
  171.4 3.6 all-to-all-done.1
  175.0 4.0 all-to-all-start
  179.1 3.1 collective-permute-start.5
  182.3 4.1 all-to-all-done
  186.4 4.7 all-to-all-start.2
  192.2 3.0 collective-permute-start.6
  209.7 5.9 %mul.135 = f32[32,64,8,64]{3,2,1,0:T(8,128)} broadcast(f32[32,64,8]{2,1,0:T(8,128)} %copy.92), dimensions={0,1,2} | broadcast | bytes 4259840 | tf_op jit(solution)/shard_map/mul | solution.py:166
  215.7 7.5 %mul.136 = f32[32,1,64,512]{3,2,1,0:T(8,128)} reshape(f32[32,64,8,64]{3,2,1,0:T(8,128)} %mul.135) | data formatting | bytes 8388608 | tf_op jit(solution)/shard_map/mul | solution.py:166
  223.2 3.6 multiply_reduce_fusion
  238.3 60.7 %all-reduce.3.cloned.1.call-done = f32[64,2880]{1,0:T(8,128)} async-done(((f32[64,2880]{1,0:T(8,128)}), f32[64,2880]{1,0:T(8,128)}) %all-reduce.3.cloned.1.call-update) | async-done | bytes 737296 | tf_op jit(solution)/shard_map/psum | solution.py:179
  301.3 2.7 convolution_convert_fusion.1
  304.0 4.6 copy.103
  308.5 50.3 %all_to_all.25 = bf16[32,16,2880]{2,1,0:T(8,128)(2,1)S(1)} all-to-all(bf16[32,16,2880]{2,1,0:T(8,128)(2,1)} %bitcast.319), channel_id=1, replica_groups=mesh['seq'=32,'tp'=8] {'seq'}, dimensions={0} | all-to-all | bytes 5898240 | tf_op jit(solution)/shard_map/all_to_all | solution.py:210
  360.4 4.2 fusion.27
  364.7 8.5 %convolution_convert_fusion = bf16[32,16,2880]{2,1,0:T(8,128)(2,1)} fusion(bf16[1,360,2880]{2,1,0:T(8,128)(2,1)} %param.32, bf16[32,16,2880]{2,1,0:T(8,128)(2,1)} %copy-done.2, bf16[1,2,2880,360]{2,3,1,0:T(8,128)(2,1)} %param.31, f32[32,1,16,360]{3,2,0,1:T(8,128)} %fusion.27), kind=kOutput, calls=%fused_computation.41 | convolution fusion | flops 2126315520 | bytes 10989568 | tf_op jit(solution)/shard_map/sexf,efd->sexd/dot_general | solution.py:88
  373.2 21.4 %copy.108 = bf16[32,16,2880]{1,0,2:T(8,128)(2,1)} copy(bf16[32,16,2880]{2,1,0:T(8,128)(2,1)} %convolution_convert_fusion) | data formatting | bytes 5898240
  394.5 39.5 %reshape.807 = bf16[2880,512]{1,0:T(8,128)(2,1)} reshape(bf16[2880,32,16]{2,1,0:T(8,128)(2,1)} %bitcast.316) | data formatting | bytes 5898240
  435.7 22.6 %all_gather.7 = bf16[32,16,1,128]{3,1,2,0:T(8,128)(2,1)S(1)} all-gather(bf16[1,16,1,128]{3,1,2,0:T(8,128)(2,1)S(1)} %bitcast_select_fusion.2), channel_id=1, replica_groups=mesh['seq'=32,'tp'=8] {'seq'}, dimensions={0}, use_global_device_ids=true | all-gather | bytes 135168 | tf_op jit(solution)/shard_map/all_gather | solution.py:227
  458.5 12.3 %reduce-scatter.4.cloned.1.call-done = bf16[360,512]{1,0:T(8,128)(2,1)} async-done(((bf16[2880,512]{1,0:T(8,128)(2,1)}), bf16[360,512]{1,0:T(8,128)(2,1)}) %reduce-scatter.4.cloned.1.call-update) | async-done | bytes 368656
  470.8 4.4 reshape.808
  475.1 5.0 copy.109
  480.2 11.2 %all-to-all-start.4 = ((bf16[32,16,360]{2,1,0:T(8,128)(2,1)}), bf16[32,16,360]{2,1,0:T(8,128)(2,1)S(1)}, u32[]{:S(2)}, u32[]{:S(2)}) async-start(bf16[32,16,360]{2,1,0:T(8,128)(2,1)} %copy.109), calls=%async_computation.4 | async-start | bytes 786432 | tf_op jit(solution)/shard_map/all_to_all | solution.py:217
  492.8 8.7 %all-to-all-done.4 = bf16[32,16,360]{2,1,0:T(8,128)(2,1)S(1)} async-done(((bf16[32,16,360]{2,1,0:T(8,128)(2,1)}), bf16[32,16,360]{2,1,0:T(8,128)(2,1)S(1)}, u32[]{:S(2)}, u32[]{:S(2)}) %all-to-all-start.4) | async-done | bytes 368672 | tf_op jit(solution)/shard_map/all_to_all | solution.py:217
  (195 shorter events, 98.6 us)
Async XLA Ops:
  7.2 219.6 %copy-start = (bf16[512,2880]{0,1:T(8,128)(2,1)S(1)}, bf16[512,2880]{0,1:T(8,128)(2,1)}, u32[]{:S(2)}) copy-start(bf16[512,2880]{0,1:T(8,128)(2,1)} %param.26) | copy-start | bytes 8847364
  7.2 56.5 %all-gather.2.cloned.1.call-start = ((), (), s32[]{:S(2)}) async-start(), calls=%async_computation.6 | async-start | bytes 2162688 | tf_op jit(solution)/shard_map/all_gather | solution.py:118
  7.9 16.3 %collective-permute-start = (bf16[64,360]{1,0:T(8,128)(2,1)}, bf16[64,360]{1,0:T(8,128)(2,1)}, u32[]{:S(2)}, u32[]{:S(2)}) collective-permute-start(bf16[64,360]{1,0:T(8,128)(2,1)} %param.27), channel_id=1, source_target_pairs={{0,1},{1,2},{2,3},{3,4},{4,5},{5,6},{6,7},{7,0},{8,9},{9,10},{10,1... | collective-permute-start | bytes 138248 | tf_op jit(solution)/shard_map/ppermute | solution.py:24
  10.5 168.7 %collective-permute-start.4 = (bf16[64,360]{1,0:T(8,128)(2,1)}, bf16[64,360]{1,0:T(8,128)(2,1)}, u32[]{:S(2)}, u32[]{:S(2)}) collective-permute-start(bf16[64,360]{1,0:T(8,128)(2,1)} %param.27), channel_id=1, source_target_pairs={{1,0},{2,1},{3,2},{4,3},{5,4},{6,5},{7,6},{0,7},{9,8},{10,9},{11,1... | collective-permute-start | bytes 138248 | tf_op jit(solution)/shard_map/ppermute | solution.py:26
  24.2 144.3 %collective-permute-start.1 = (bf16[64,360]{1,0:T(8,128)(2,1)}, bf16[64,360]{1,0:T(8,128)(2,1)}, u32[]{:S(2)}, u32[]{:S(2)}) collective-permute-start(bf16[64,360]{1,0:T(8,128)(2,1)} %collective-permute-done), channel_id=1, source_target_pairs={{0,1},{1,2},{2,3},{3,4},{4,5},{5,6},{6,7},{7,0},{8,9},{9,10},{10,1... | collective-permute-start | bytes 138248 | tf_op jit(solution)/shard_map/ppermute | solution.py:24
  78.0 2.9 copy-start.1
  102.3 2.9 copy-start.1
  126.6 2.9 copy-start.1
  150.9 3.0 copy-start.1
  160.9 30.3 %copy-start.4 = (f32[1,64,1,8,64]{4,1,3,2,0:T(8,128)S(1)}, f32[1,64,1,8,64]{4,1,3,2,0:T(8,128)}, u32[]{:S(2)}) copy-start(f32[1,64,1,8,64]{4,1,3,2,0:T(8,128)} %convolution_bitcast_fusion) | copy-start | bytes 393220
  162.6 12.4 %all-to-all-start.1 = ((f32[32,1,512]{2,1,0:T(1,128)}), f32[32,1,512]{2,1,0:T(1,128)S(1)}, u32[]{:S(2)}, u32[]{:S(2)}) async-start(f32[32,1,512]{2,1,0:T(1,128)} %reshape.812), calls=%async_computation.1 | async-start | bytes 131072 | tf_op jit(solution)/shard_map/all_to_all | solution.py:133
  168.5 13.8 %collective-permute-start.2 = (bf16[64,360]{1,0:T(8,128)(2,1)}, bf16[64,360]{1,0:T(8,128)(2,1)}, u32[]{:S(2)}, u32[]{:S(2)}) collective-permute-start(bf16[64,360]{1,0:T(8,128)(2,1)} %collective-permute-done.1), channel_id=1, source_target_pairs={{0,1},{1,2},{2,3},{3,4},{4,5},{5,6},{6,7},{7,0},{8,9},{9,10},{10,1... | collective-permute-start | bytes 138248 | tf_op jit(solution)/shard_map/ppermute | solution.py:24
  175.0 11.4 %all-to-all-start = ((f32[32,1,512]{2,1,0:T(1,128)}), f32[32,1,512]{2,1,0:T(1,128)S(1)}, u32[]{:S(2)}, u32[]{:S(2)}) async-start(f32[32,1,512]{2,1,0:T(1,128)} %reshape.810), calls=%async_computation | async-start | bytes 131072 | tf_op jit(solution)/shard_map/all_to_all | solution.py:134
  179.1 13.1 %collective-permute-start.5 = (bf16[64,360]{1,0:T(8,128)(2,1)}, bf16[64,360]{1,0:T(8,128)(2,1)}, u32[]{:S(2)}, u32[]{:S(2)}) collective-permute-start(bf16[64,360]{1,0:T(8,128)(2,1)} %collective-permute-done.4), channel_id=1, source_target_pairs={{1,0},{2,1},{3,2},{4,3},{5,4},{6,5},{7,6},{0,7},{9,8},{10,9},{11,1... | collective-permute-start | bytes 138248 | tf_op jit(solution)/shard_map/ppermute | solution.py:26
  182.3 12.9 %collective-permute-start.3 = (bf16[64,360]{1,0:T(8,128)(2,1)}, bf16[64,360]{1,0:T(8,128)(2,1)}, u32[]{:S(2)}, u32[]{:S(2)}) collective-permute-start(bf16[64,360]{1,0:T(8,128)(2,1)} %collective-permute-done.2), channel_id=1, source_target_pairs={{0,1},{1,2},{2,3},{3,4},{4,5},{5,6},{6,7},{7,0},{8,9},{9,10},{10,1... | collective-permute-start | bytes 138248 | tf_op jit(solution)/shard_map/ppermute | solution.py:24
  186.4 4.8 copy-start.9
  186.4 36.7 %all-to-all-start.2 = ((bf16[32,1,64,512]{3,2,1,0:T(8,128)(2,1)}), bf16[32,1,64,512]{3,2,1,0:T(8,128)(2,1)}, u32[]{:S(2)}, u32[]{:S(2)}) async-start(bf16[32,1,64,512]{3,2,1,0:T(8,128)(2,1)} %bitcast.323), calls=%async_computation.2 | async-start | bytes 4194304 | tf_op jit(solution)/shard_map/all_to_all | solution.py:131
  191.2 107.8 %all-reduce.3.cloned.1.call-start = ((), (), s32[]{:S(2)}) async-start(), calls=%async_computation.7 | async-start | bytes 1507328 | tf_op jit(solution)/shard_map/psum | solution.py:179
  192.2 39.4 %collective-permute-start.6 = (bf16[64,360]{1,0:T(8,128)(2,1)}, bf16[64,360]{1,0:T(8,128)(2,1)}, u32[]{:S(2)}, u32[]{:S(2)}) collective-permute-start(bf16[64,360]{1,0:T(8,128)(2,1)} %collective-permute-done.5), channel_id=1, source_target_pairs={{1,0},{2,1},{3,2},{4,3},{5,4},{6,5},{7,6},{0,7},{9,8},{10,9},{11,1... | collective-permute-start | bytes 138248 | tf_op jit(solution)/shard_map/ppermute | solution.py:26
  223.1 3.6 copy-start.6
  223.1 3.6 copy-start.7
  228.7 242.1 %reduce-scatter.4.cloned.1.call-start = ((), (), s32[]{:S(2)}) async-start(), calls=%async_computation.8 | async-start | bytes 3317760
  234.6 66.7 %copy-start.5 = (s32[512,64]{0,1:T(8,128)S(1)}, s32[512,64]{0,1:T(8,128)}, u32[]{:S(2)}) copy-start(s32[512,64]{0,1:T(8,128)} %convert_reduce_fusion) | copy-start | bytes 393220
  234.6 66.7 %copy-start.11 = (f32[2880]{0:T(1024)S(1)}, f32[2880]{0:T(1024)}, u32[]{:S(2)}) copy-start(f32[2880]{0:T(1024)} %param.28) | copy-start | bytes 34564
  300.5 0.8 copy-start.3
  358.8 1.6 copy-start.2
  394.5 39.5 %copy-start.10 = (s32[64,4]{0,1:T(4,128)S(1)}, s32[64,4]{0,1:T(4,128)}, u32[]{:S(2)}) copy-start(s32[64,4]{0,1:T(4,128)} %param.29) | copy-start | bytes 3076
  434.0 0.9 copy-start.15
  434.0 1.0 copy-start.8
  434.0 24.3 %copy-start.14 = (s32[32]{0:T(128)S(1)}, s32[32]{0:T(128)}, u32[]{:S(2)}) copy-start(s32[32]{0:T(128)} %param.35) | copy-start | bytes 388
  458.5 33.0 %copy-start.13 = (pred[64,4]{0,1:T(4,128)(4,1)S(1)}, pred[64,4]{0,1:T(4,128)(4,1)}, u32[]{:S(2)}) copy-start(pred[64,4]{0,1:T(4,128)(4,1)} %get-tuple-element.131) | copy-start | bytes 772
  458.5 33.1 %copy-start.12 = (f32[64,4]{0,1:T(4,128)S(1)}, f32[64,4]{0,1:T(4,128)}, u32[]{:S(2)}) copy-start(f32[64,4]{0,1:T(4,128)} %param.30) | copy-start | bytes 3076
  480.2 21.4 %all-to-all-start.4 = ((bf16[32,16,360]{2,1,0:T(8,128)(2,1)}), bf16[32,16,360]{2,1,0:T(8,128)(2,1)S(1)}, u32[]{:S(2)}, u32[]{:S(2)}) async-start(bf16[32,16,360]{2,1,0:T(8,128)(2,1)} %copy.109), calls=%async_computation.4 | async-start | bytes 786432 | tf_op jit(solution)/shard_map/all_to_all | solution.py:217
Sparse Core Ops, SparseCore 0:
  10.6 53.0 all-gather.1
  228.8 70.1 all-reduce.2
  434.2 36.5 reduce-scatter.3
